TPU v7x, 32 devices: a whole 2x2x4 slice. The times are simulated.
32 devices in a mesh: cuts: 2 (over y), wide: 8 (over z, x), narrow: 2 (over core).
Axes of the slice: x: 2, y: 2, z: 4, core: 2. Of those that a mesh axis runs over, the one named last changes fastest.
Arguments:
- stem_tensor: float32 [2, 4194304], P(None, ('cuts', 'wide', 'narrow')), parts along dimension 1, may hold values from -6 to 6
- sub_branches: bfloat16 [3, 2, 2, 512, 512], P(None, 'narrow', None, 'wide'), may hold values from -0.1875 to 0.1875
- branch_bits: int32 [3, 9], replicated, may hold values from 7 to 20, as said below
Outputs:
- amplitudes: float32 [2, 4194304], P(None, ('cuts', 'wide', 'narrow')), parts along dimension 1
There are 2 independent parts, one for each index of `cuts`. A program takes and returns all parts, laid end to end along the dimension named above; an argument that names none is the same for every part. Nothing has to cross between parts.
Inputs may be any that keep to these rules, and one draw needn't show every extreme that they name: `branch_bits`: no bit below 7 is ever named. Row 0 holds 9 distinct bits of 7 to 16, bit 7 among them. Row 1 holds the 3 bits 17 + 1 to 20 and 6 distinct bits of 7 to 12. Row 2 holds bit 17 and 8 distinct bits of 7 to 12 and 18 to 20. Each row in any order.
All inputs are finite; a program needn't handle non-finite values.
Results may differ from a plain program's by a relative error of at most 0.005.
Values may be sent and summed in bfloat16 or wider, within the bound.
A program may use at most 64 MiB of HBM per device.

v0:
```python
import functools

import jax
import jax.numpy as jnp
from jax import lax
from jax.experimental import pallas as pl
from jax.experimental.pallas import tpu as pltpu
from jax.sharding import PartitionSpec as P

LBITS = 17
BBITS = 9
BRANCHES = 3


lane_bits = 7


def partner(value, axis, stride):
    mask = 2**stride
    pairs = [(source, source ^ mask) for source in range(lax.axis_size(axis))]
    return lax.ppermute(value, axis, pairs)


def bit_tables(chosen_bits, total_bits, width_bits):
    places = jnp.arange(total_bits, dtype=jnp.int32)
    orders = jnp.arange(width_bits, dtype=jnp.int32)
    matches = places[:, None] == chosen_bits[None, :]
    chosen = jnp.any(matches, axis=1)
    ranking = jnp.sum(jnp.where(matches, orders[None, :], 0), axis=1)
    unchosen = 1 - chosen.astype(jnp.int32)
    free_rank = jnp.cumsum(unchosen) - unchosen
    unit_ones = jnp.ones((total_bits,), jnp.int32)
    weight = jnp.where(
        chosen,
        jnp.left_shift(unit_ones, width_bits - 1 - ranking),
        jnp.left_shift(unit_ones, width_bits + free_rank),
    )
    low_bits = total_bits // 2

    def partial_table(count, first_place, last_place):
        values = jnp.arange(count, dtype=jnp.int32)
        running = jnp.zeros((count,), jnp.int32)
        for position in range(first_place, last_place):
            running = (
                running
                + jnp.bitwise_and(jnp.right_shift(values, position - first_place), 1)
                * weight[position]
            )
        return running

    inverse = (
        partial_table(2 ** (total_bits - low_bits), low_bits, total_bits)[:, None]
        + partial_table(2**low_bits, 0, low_bits)[None, :]
    ).reshape(-1)
    columns = jnp.arange(2**width_bits, dtype=jnp.int32)
    col_part = jnp.zeros((2**width_bits,), jnp.int32)
    for slot_no in range(width_bits):
        col_part = col_part + jnp.left_shift(
            jnp.bitwise_and(jnp.right_shift(columns, width_bits - 1 - slot_no), 1),
            chosen_bits[slot_no],
        )
    row_ids = jnp.arange(2 ** (total_bits - width_bits), dtype=jnp.int32)
    row_part = jnp.zeros((2 ** (total_bits - width_bits),), jnp.int32)
    for position in range(total_bits):
        bit_value = jnp.bitwise_and(jnp.right_shift(row_ids, free_rank[position]), 1) * 2**position
        row_part = row_part + jnp.where(chosen[position], 0, bit_value)
    gather_index = row_part[:, None] + col_part[None, :]
    return (gather_index, inverse)


def half_product(first_matrix, second_matrix):
    return jnp.dot(first_matrix, second_matrix, preferred_element_type=jnp.float32)


def merge_branch(left_factor, right_factor):
    real_part = half_product(left_factor[0], right_factor[0]) - half_product(
        left_factor[1], right_factor[1]
    )
    imag_part = half_product(left_factor[0], right_factor[1]) + half_product(
        left_factor[1], right_factor[0]
    )
    return jnp.stack([real_part, imag_part]).astype(jnp.bfloat16)


def contract_blocks(amplitude, branch, gather_index, inverse):
    lanes = 2**lane_bits
    blocks = amplitude.reshape(2, -1, lanes)
    picked = jnp.take(blocks, gather_index, axis=1)
    widened = branch.astype(jnp.float32)

    def real_product(data, matrix):
        return jnp.einsum(
            "rul,cu->rcl",
            data,
            matrix,
            precision=lax.Precision.HIGHEST,
            preferred_element_type=jnp.float32,
        )

    real_part = real_product(picked[0], widened[0]) - real_product(picked[1], widened[1])
    imag_part = real_product(picked[0], widened[1]) + real_product(picked[1], widened[0])
    merged = jnp.stack([real_part, imag_part]).reshape(2, -1, lanes)
    return jnp.take(merged, inverse, axis=1).reshape(2, -1)


def shards(stem_tensor, sub_branches, branch_bits):
    wide_count = lax.axis_size("wide")
    wide_log = wide_count.bit_length() - 1
    local_bits = LBITS
    block_shape = (2, wide_count, 2, stem_tensor.shape[1] // (2 * wide_count))
    leading = lax.axis_index("narrow") == 0

    def move_wide(amplitude):
        return lax.all_to_all(
            amplitude.reshape(block_shape), "wide", split_axis=1, concat_axis=1, tiled=True
        ).reshape(2, -1)

    def move_narrow(amplitude):
        return lax.all_to_all(
            amplitude.reshape(block_shape), "narrow", split_axis=2, concat_axis=2, tiled=True
        ).reshape(2, -1)

    def working_places(which):
        chosen_bits = branch_bits[which]
        if which == 0:
            return chosen_bits - lane_bits
        shifted = jnp.where(chosen_bits == local_bits, local_bits - wide_log - 1, chosen_bits)
        placed = jnp.where(chosen_bits > local_bits, chosen_bits - wide_log - 1, shifted)
        return placed - lane_bits

    amplitude = stem_tensor
    for which in range(BRANCHES):
        own_rows = sub_branches[which, 0]
        own_whole = lax.all_gather(own_rows, "wide", axis=1, tiled=True)
        partner_whole = partner(own_whole, "narrow", 0)
        branch = merge_branch(
            jnp.where(leading, own_whole, partner_whole),
            jnp.where(leading, partner_whole, own_whole),
        )
        if which == 1:
            amplitude = move_wide(amplitude)
        if which == 2:
            amplitude = move_narrow(amplitude)
        gather_index, inverse = bit_tables(working_places(which), local_bits - lane_bits, BBITS)
        amplitude = contract_blocks(amplitude, branch, gather_index, inverse)
    amplitude = move_narrow(amplitude)
    amplitude = move_wide(amplitude)
    return amplitude


MESH = pl.DeviceIdType.MESH


def stem_kernel(
    count, places_ref, stem_ref, sub_ref, out_ref,
    gath, bcat, work, prod, send, recv, stem_held,
    stem_sem, own_sem, z_send, z_recv, x_send, x_recv, y_send, y_recv,
    pair_send, pair_recv, swap_send, swap_recv,
):
    wide = lax.axis_index("wide")
    narrow = lax.axis_index("narrow")
    cut = lax.axis_index("cuts")
    rows = sub_ref.shape[2]
    branches = sub_ref.shape[0]
    dim = bcat.shape[1]
    total = work.shape[0]
    lanes = work.shape[1] // 2
    bits = total.bit_length() - 1
    depth = count // 2
    z = wide // 2
    x = wide % 2
    members = 2 * count
    me = wide * 2 + narrow
    piece = total // members

    stem_copy = pltpu.make_async_copy(stem_ref, stem_held, stem_sem)
    stem_copy.start()
    barrier = pltpu.get_barrier_semaphore()
    for target in ({"wide": 2 * z + 1 - x}, {"cuts": 1 - cut}, {"narrow": 1 - narrow}):
        pl.semaphore_signal(barrier, inc=1, device_id=target, device_id_type=MESH)

    @pl.when(z + 1 < depth)
    def _():
        pl.semaphore_signal(barrier, inc=1, device_id={"wide": wide + 2}, device_id_type=MESH)

    @pl.when(z > 0)
    def _():
        pl.semaphore_signal(barrier, inc=1, device_id={"wide": wide - 2}, device_id_type=MESH)

    pl.semaphore_wait(barrier, 3 + jnp.minimum(z, 1) + jnp.minimum(depth - 1 - z, 1))

    started = []
    own_copies = []

    def there(way, distance):
        return z >= distance if way == 0 else z + distance < depth

    def level(way, distance):
        return z - distance if way == 0 else z + distance

    def slot_of(way, distance):
        return 0 if distance == 0 else 1 + way * (depth - 1) + distance - 1

    def part_of(side):
        return cut if side == 0 else 1 - cut

    def copy_of(which, side, column, way, distance, send_sem, recv_sem, device_id):
        origin = 2 * level(way, distance) + (x if column == 0 else 1 - x)
        span = pl.ds(pl.multiple_of(origin * rows, rows), rows)
        target = gath.at[narrow, which, part_of(side), span]
        own = distance == 0 and column == 0
        return pltpu.make_async_remote_copy(
            src_ref=sub_ref.at[which, part_of(side)] if own else target,
            dst_ref=target,
            send_sem=send_sem,
            recv_sem=recv_sem,
            device_id=device_id,
            device_id_type=MESH,
        )

    def z_copy(which, side, way, distance):
        slot = depth - 1 if side == 1 else distance - 1
        return copy_of(
            which, side, 0, way, distance - 1,
            z_send.at[way, which, slot], z_recv.at[way, which, slot],
            {"wide": wide + 2 if way == 0 else wide - 2},
        )

    def x_copy(which, side, way, distance):
        slot = side if distance == 0 else 1 + slot_of(way, distance)
        return copy_of(
            which, side, 0, way, distance,
            x_send.at[which, slot], x_recv.at[which, slot], {"wide": 2 * z + 1 - x},
        )

    def y_copy(which, column, way, distance):
        slot = slot_of(way, distance)
        return copy_of(
            which, 0, column, way, distance,
            y_send.at[which, column, slot], y_recv.at[which, column, slot],
            {"cuts": 1 - cut},
        )

    def pair_copy(which, side, column, way, distance):
        slot = slot_of(way, distance)
        return copy_of(
            which, side, column, way, distance,
            pair_send.at[which, side, column, slot], pair_recv.at[which, side, column, slot],
            {"narrow": 1 - narrow},
        )

    def launch(build, guard=None):
        if guard is None:
            build().start()
        else:
            pl.when(guard)(lambda: build().start())
        started.append((build, guard))

    def finish(build, guard):
        if guard is None:
            build().wait_send()
        else:
            pl.when(guard)(lambda: build().wait_send())

    def await_recv(build, guard=None):
        if guard is None:
            build().wait_recv()
        else:
            pl.when(guard)(lambda: build().wait_recv())

    ways = (0, 1)
    part_sides = (0, 1)
    call = functools.partial

    def send_own_z(which):
        for way in ways:
            launch(call(z_copy, which, 0, way, 1), there(1 - way, 1))

    def send_own_x(which):
        for side in part_sides:
            launch(call(x_copy, which, side, 0, 0))
        for side in part_sides:
            launch(call(pair_copy, which, side, 0, 0, 0))
            origin = pl.ds(pl.multiple_of(wide * rows, rows), rows)
            keep = pltpu.make_async_copy(
                sub_ref.at[which, side], gath.at[narrow, which, side, origin],
                own_sem.at[which, side],
            )
            keep.start()
            own_copies.append(keep)

    def take_x_own(which):
        for side in part_sides:
            await_recv(call(x_copy, which, side, 0, 0))
            launch(call(pair_copy, which, side, 1, 0, 0))

    def take_z(which, distance):
        for way in ways:
            guard = there(way, distance)
            await_recv(call(z_copy, which, 0, way, distance), guard)
            if distance + 1 < depth:
                launch(
                    call(z_copy, which, 0, way, distance + 1),
                    jnp.logical_and(guard, there(1 - way, 1)),
                )
            launch(call(y_copy, which, 0, way, distance), guard)
            launch(call(x_copy, which, 0, way, distance), guard)
            launch(call(pair_copy, which, 0, 0, way, distance), guard)

    def take_x(which, distance):
        for way in ways:
            guard = there(way, distance)
            await_recv(call(x_copy, which, 0, way, distance), guard)
            launch(call(y_copy, which, 1, way, distance), guard)
            launch(call(pair_copy, which, 0, 1, way, distance), guard)

    def take_y(which, distance):
        for way in ways:
            guard = there(way, distance)
            for column in (0, 1):
                await_recv(call(y_copy, which, column, way, distance), guard)
                launch(call(pair_copy, which, 1, column, way, distance), guard)

    def complete(which):
        for side in part_sides:
            own_copies[2 * which + side].wait()
            for column in (0, 1):
                await_recv(call(pair_copy, which, side, column, 0, 0))
                for way in ways:
                    for distance in range(1, depth):
                        await_recv(
                            call(pair_copy, which, side, column, way, distance),
                            there(way, distance),
                        )

    def advance(slot):
        for which in range(branches):
            distance = slot - which
            if 1 <= distance < depth:
                take_z(which, distance)
            if distance == 1 and which + 1 < branches:
                send_own_z(which + 1)
            if 1 <= distance - 1 < depth:
                take_x(which, distance - 1)
            if distance == 2:
                take_x_own(which)
                if which + 1 < branches:
                    send_own_x(which + 1)
            if which == 0 and 1 <= distance - 2 < depth:
                take_y(which, distance - 2)

    def take_mates(which):
        for distance in range(1, depth):
            take_y(which, distance)

    def merge(which):
        held = bcat.at[which % 2]
        first = [gath[0, which, part] for part in range(2)]
        second = [gath[1, which, part] for part in range(2)]

        def half_product(left, right):
            return jnp.dot(left, right, preferred_element_type=jnp.float32)

        held[:, :dim] = (
            half_product(first[0], second[0]) - half_product(first[1], second[1])
        ).astype(jnp.bfloat16)
        held[:, dim:] = (
            half_product(first[0], second[1]) + half_product(first[1], second[0])
        ).astype(jnp.bfloat16)

    width = dim.bit_length() - 1

    narrow_place = bits - 1 - (count.bit_length() - 1)

    def named_place(which, slot):
        bit = places_ref[which, slot]
        return bit + jnp.where(bit < LBITS, -lane_bits, narrow_place - LBITS)

    places = [[named_place(which, slot) for slot in range(width)] for which in range(branches)]

    def free_place(which):
        rest = bits * (bits - 1) // 2
        for slot in range(width):
            rest = rest - places[which][slot]
        return rest

    def bit_at(values, position):
        return jnp.bitwise_and(jnp.right_shift(values, position), 1)

    def gathered_place(which, values):
        found = jnp.left_shift(bit_at(values, free_place(which)), width)
        for slot in range(width):
            found = found + jnp.left_shift(
                bit_at(values, places[which][slot]), width - 1 - slot
            )
        return found

    def natural_place(which, values):
        found = jnp.left_shift(bit_at(values, width), free_place(which))
        for slot in range(width):
            found = found + jnp.left_shift(
                bit_at(values, width - 1 - slot), places[which][slot]
            )
        return found

    def permute(source, target_ref, goal):
        step = min(256, total)
        for first in range(0, total, step):
            index = lax.broadcasted_iota(jnp.int32, (step, total), 0) + first
            onehot = (index == goal).astype(jnp.float32).astype(jnp.bfloat16)
            target_ref[first:first + step, :] = jnp.dot(
                onehot, source, preferred_element_type=jnp.float32
            ).astype(jnp.bfloat16)

    def contract(which):
        for first in range(0, total, dim):
            data = work[first:first + dim, :]
            turned = jnp.concatenate([-data[:, lanes:], data[:, :lanes]], axis=1)
            both = jnp.concatenate([data, turned], axis=0)
            prod[first:first + dim, :] = jnp.dot(
                bcat[which % 2], both, preferred_element_type=jnp.float32
            ).astype(jnp.bfloat16)

    far_first = sorted(range(depth), key=lambda hop: -min(hop, depth - hop))
    level_rows = total // depth

    def swap_targets(round_no, hop):
        level_z = (z + hop) % depth
        for turn in range(4):
            across, other_core = turn // 2, turn % 2
            if hop == 0 and turn == 0:
                continue
            to_x = x if across == 0 else 1 - x
            to_core = narrow if other_core == 0 else 1 - narrow
            to_wide = 2 * level_z + to_x
            other = 2 * to_wide + to_core
            yield pltpu.make_async_remote_copy(
                src_ref=send.at[round_no, pl.ds(pl.multiple_of(other * piece, piece), piece)],
                dst_ref=recv.at[round_no, pl.ds(pl.multiple_of(me * piece, piece), piece)],
                send_sem=swap_send.at[round_no, 4 * hop + turn],
                recv_sem=swap_recv.at[round_no, 4 * hop + turn],
                device_id={"wide": to_wide, "narrow": to_core},
                device_id_type=MESH,
            )

    def swap_level(round_no, hop, source, goal):
        first = ((z + hop) % depth) * level_rows
        index = lax.broadcasted_iota(jnp.int32, (level_rows, total), 0) + first
        onehot = (index == goal).astype(jnp.float32).astype(jnp.bfloat16)
        send[round_no, pl.ds(pl.multiple_of(first, level_rows), level_rows), :] = jnp.dot(
            onehot, source, preferred_element_type=jnp.float32
        ).astype(jnp.bfloat16)
        for copy in swap_targets(round_no, hop):
            copy.start()

    def swap_out(round_no, goal):
        source = prod[...]
        for hop in far_first:
            swap_level(round_no, hop, source, goal)
        mine = pl.ds(pl.multiple_of(me * piece, piece), piece)
        recv[round_no, mine, :] = send[round_no, mine, :]

    def swap_wait(round_no):
        for hop in far_first:
            for copy in swap_targets(round_no, hop):
                copy.wait_recv()

    line = lax.broadcasted_iota(jnp.int32, (1, total), 1)
    send_own_z(0)
    send_own_x(0)
    stem_copy.wait()
    stem = jnp.concatenate(
        [stem_held[pl.ds(part, total, stride=2), :] for part in range(2)], axis=1
    ).astype(jnp.bfloat16)
    permute(stem, work, gathered_place(0, line))
    for slot in range(1, depth + 2):
        advance(slot)
    complete(0)
    merge(0)
    contract(0)
    swap_out(0, natural_place(0, line))
    for slot in range(depth + 2, depth + branches):
        advance(slot)
    take_mates(1)
    complete(1)
    merge(1)
    take_mates(2)
    complete(2)
    merge(2)
    swap_wait(0)
    permute(recv[0], work, gathered_place(1, line))
    contract(1)
    permute(prod[...], work, gathered_place(2, natural_place(1, line)))
    contract(2)
    swap_out(1, natural_place(2, line))
    swap_wait(1)
    for part in range(2):
        out_ref[pl.ds(part, total, stride=2), :] = recv[
            1, :, part * lanes:(part + 1) * lanes
        ].astype(jnp.float32)
    for round_no in range(2):
        for hop in range(depth):
            for copy in swap_targets(round_no, hop):
                copy.wait_send()
    for build, guard in started:
        finish(build, guard)


def shards_in_kernel(stem_tensor, sub_branches, branch_bits):
    count = lax.axis_size("wide")
    depth = count // 2
    lanes = 2**lane_bits
    total = stem_tensor.shape[1] // lanes
    dim = sub_branches.shape[-1]
    stem = stem_tensor.reshape(2, total, lanes).transpose(1, 0, 2).reshape(2 * total, lanes)
    vmem = pl.BlockSpec(memory_space=pltpu.VMEM)
    hbm = pl.BlockSpec(memory_space=pl.ANY)
    slots = 2 * depth - 1
    semaphores = [(BRANCHES, 2)]
    for shape in ((2, BRANCHES, depth), (BRANCHES, slots + 1), (BRANCHES, 2, slots),
                  (BRANCHES, 2, 2, slots), (2, 2 * count)):
        semaphores += [shape, shape]
    result = pl.pallas_call(
        functools.partial(stem_kernel, count),
        out_shape=jax.ShapeDtypeStruct((2 * total, lanes), jnp.float32),
        in_specs=[pl.BlockSpec(memory_space=pltpu.SMEM), hbm, hbm],
        out_specs=vmem,
        scratch_shapes=[
            pltpu.VMEM((2, BRANCHES, 2, dim, dim), jnp.bfloat16),
            pltpu.VMEM((2, dim, 2 * dim), jnp.bfloat16),
            pltpu.VMEM((total, 2 * lanes), jnp.bfloat16),
            pltpu.VMEM((total, 2 * lanes), jnp.bfloat16),
            pltpu.VMEM((2, total, 2 * lanes), jnp.bfloat16),
            pltpu.VMEM((2, total, 2 * lanes), jnp.bfloat16),
            pltpu.VMEM((2 * total, lanes), jnp.float32),
            pltpu.SemaphoreType.DMA(()),
        ] + [pltpu.SemaphoreType.DMA(shape) for shape in semaphores],
        compiler_params=pltpu.CompilerParams(collective_id=0, has_side_effects=True),
    )(branch_bits, stem, sub_branches[:, 0])
    return result.reshape(total, 2, lanes).transpose(1, 0, 2).reshape(2, -1)


sublane_tile = 16


def solution(mesh):
    in_specs = (P(None, ("cuts", "wide", "narrow")), P(None, "narrow", None, "wide", None), P())
    out_specs = P(None, ("cuts", "wide", "narrow"))

    def run(stem_tensor, sub_branches, branch_bits):
        whole_tiles = sub_branches.shape[3] % sublane_tile == 0 and mesh.shape["cuts"] == 2
        body = shards_in_kernel if whole_tiles else shards
        return body(stem_tensor, sub_branches, branch_bits)

    return jax.shard_map(run, mesh=mesh, in_specs=in_specs, out_specs=out_specs, check_vma=False)
```

profile of v0, /device:TPU:9, one launch (start us, length us, event | category | flops | bytes accessed | tf_op | source)
XLA Modules:
  0.0 63.3 jit_solution(11138421894245121469)
XLA Ops:
  0.0 61.0 %shard_map.37 = f32[2048,128]{1,0:T(8,128)} custom-call(s32[3,9]{1,0:T(4,128)} %places_ref.1, f32[2048,128]{1,0:T(8,128)} %bitcast.12, bf16[3,2,64,512]{3,2,1,0:T(8,128)(2,1)} %bitcast.13), custom_call_target="tpu_custom_call" | custom-call | tf_op jit(solution)/shard_map/pallas_call | solution.py:523
  61.1 2.3 %copy.7 = f32[2,131072]{1,0:T(2,128)} copy(f32[2,131072]{1,0:T(2,128)} %bitcast.11) | data formatting | bytes 2097152
where the time goes:
time: 63.5 us; the launch traced here: 63.3 us
  Pallas kernels  61 us (96%)
  local copies, waits for them, and re-layouts  2.26 us (4%)
    pallas_call x1, Pallas kernels, shards_in_kernel(): pl.pallas_call(functools.partial(stem_kernel, count), out_shape=jax.Shape...  61 us
    unnamed x1, local copies, waits for them, and re-layouts  2.26 us

commit v1 on v0

v1 whole, which is shorter than its diff:
```python
import functools

import jax
import jax.numpy as jnp
from jax import lax
from jax.experimental import pallas as pl
from jax.experimental.pallas import tpu as pltpu
from jax.sharding import PartitionSpec as P

LBITS = 17
BBITS = 9
BRANCHES = 3


lane_bits = 7
sublanes = 8
CORNERS_OVER_X = ((0, 2), (2, 0), (2, 2))
WHOLE_WAY = ()


def partner(value, axis, stride):
    mask = 2**stride
    pairs = [(source, source ^ mask) for source in range(lax.axis_size(axis))]
    return lax.ppermute(value, axis, pairs)


def bit_tables(chosen_bits, total_bits, width_bits):
    places = jnp.arange(total_bits, dtype=jnp.int32)
    orders = jnp.arange(width_bits, dtype=jnp.int32)
    matches = places[:, None] == chosen_bits[None, :]
    chosen = jnp.any(matches, axis=1)
    ranking = jnp.sum(jnp.where(matches, orders[None, :], 0), axis=1)
    unchosen = 1 - chosen.astype(jnp.int32)
    free_rank = jnp.cumsum(unchosen) - unchosen
    unit_ones = jnp.ones((total_bits,), jnp.int32)
    weight = jnp.where(
        chosen,
        jnp.left_shift(unit_ones, width_bits - 1 - ranking),
        jnp.left_shift(unit_ones, width_bits + free_rank),
    )
    low_bits = total_bits // 2

    def partial_table(count, first_place, last_place):
        values = jnp.arange(count, dtype=jnp.int32)
        running = jnp.zeros((count,), jnp.int32)
        for position in range(first_place, last_place):
            running = (
                running
                + jnp.bitwise_and(jnp.right_shift(values, position - first_place), 1)
                * weight[position]
            )
        return running

    inverse = (
        partial_table(2 ** (total_bits - low_bits), low_bits, total_bits)[:, None]
        + partial_table(2**low_bits, 0, low_bits)[None, :]
    ).reshape(-1)
    columns = jnp.arange(2**width_bits, dtype=jnp.int32)
    col_part = jnp.zeros((2**width_bits,), jnp.int32)
    for slot_no in range(width_bits):
        col_part = col_part + jnp.left_shift(
            jnp.bitwise_and(jnp.right_shift(columns, width_bits - 1 - slot_no), 1),
            chosen_bits[slot_no],
        )
    row_ids = jnp.arange(2 ** (total_bits - width_bits), dtype=jnp.int32)
    row_part = jnp.zeros((2 ** (total_bits - width_bits),), jnp.int32)
    for position in range(total_bits):
        bit_value = jnp.bitwise_and(jnp.right_shift(row_ids, free_rank[position]), 1) * 2**position
        row_part = row_part + jnp.where(chosen[position], 0, bit_value)
    gather_index = row_part[:, None] + col_part[None, :]
    return (gather_index, inverse)


def half_product(first_matrix, second_matrix):
    return jnp.dot(first_matrix, second_matrix, preferred_element_type=jnp.float32)


def merge_branch(left_factor, right_factor):
    real_part = half_product(left_factor[0], right_factor[0]) - half_product(
        left_factor[1], right_factor[1]
    )
    imag_part = half_product(left_factor[0], right_factor[1]) + half_product(
        left_factor[1], right_factor[0]
    )
    return jnp.stack([real_part, imag_part]).astype(jnp.bfloat16)


def contract_blocks(amplitude, branch, gather_index, inverse):
    lanes = 2**lane_bits
    blocks = amplitude.reshape(2, -1, lanes)
    picked = jnp.take(blocks, gather_index, axis=1)
    widened = branch.astype(jnp.float32)

    def real_product(data, matrix):
        return jnp.einsum(
            "rul,cu->rcl",
            data,
            matrix,
            precision=lax.Precision.HIGHEST,
            preferred_element_type=jnp.float32,
        )

    real_part = real_product(picked[0], widened[0]) - real_product(picked[1], widened[1])
    imag_part = real_product(picked[0], widened[1]) + real_product(picked[1], widened[0])
    merged = jnp.stack([real_part, imag_part]).reshape(2, -1, lanes)
    return jnp.take(merged, inverse, axis=1).reshape(2, -1)


def shards(stem_tensor, sub_branches, branch_bits):
    wide_count = lax.axis_size("wide")
    wide_log = wide_count.bit_length() - 1
    local_bits = LBITS
    block_shape = (2, wide_count, 2, stem_tensor.shape[1] // (2 * wide_count))
    leading = lax.axis_index("narrow") == 0

    def move_wide(amplitude):
        return lax.all_to_all(
            amplitude.reshape(block_shape), "wide", split_axis=1, concat_axis=1, tiled=True
        ).reshape(2, -1)

    def move_narrow(amplitude):
        return lax.all_to_all(
            amplitude.reshape(block_shape), "narrow", split_axis=2, concat_axis=2, tiled=True
        ).reshape(2, -1)

    def working_places(which):
        chosen_bits = branch_bits[which]
        if which == 0:
            return chosen_bits - lane_bits
        shifted = jnp.where(chosen_bits == local_bits, local_bits - wide_log - 1, chosen_bits)
        placed = jnp.where(chosen_bits > local_bits, chosen_bits - wide_log - 1, shifted)
        return placed - lane_bits

    amplitude = stem_tensor
    for which in range(BRANCHES):
        own_rows = sub_branches[which, 0]
        own_whole = lax.all_gather(own_rows, "wide", axis=1, tiled=True)
        partner_whole = partner(own_whole, "narrow", 0)
        branch = merge_branch(
            jnp.where(leading, own_whole, partner_whole),
            jnp.where(leading, partner_whole, own_whole),
        )
        if which == 1:
            amplitude = move_wide(amplitude)
        if which == 2:
            amplitude = move_narrow(amplitude)
        gather_index, inverse = bit_tables(working_places(which), local_bits - lane_bits, BBITS)
        amplitude = contract_blocks(amplitude, branch, gather_index, inverse)
    amplitude = move_narrow(amplitude)
    amplitude = move_wide(amplitude)
    return amplitude


MESH = pl.DeviceIdType.MESH


def xor(first, second):
    return first + second - 2 * first * second


def stem_kernel(
    count, places_ref, stem_ref, sub_ref, out_ref,
    xbuf, ybuf, bbuf, work, prod, turned, flipped, send_in, recv_in, send_out, recv_out, stem_held,
    stem_sem, own_sem, left_send, left_recv, right_send, right_recv, pair_send, pair_recv,
    relay_send, zb_send, zb_recv, xb_send, xb_recv, yb_send, yb_recv, pb_send, pb_recv,
    swap_send, swap_recv,
):
    wide = lax.axis_index("wide")
    narrow = lax.axis_index("narrow")
    cut = lax.axis_index("cuts")
    rows = sub_ref.shape[2]
    branches = sub_ref.shape[0]
    dim = bbuf.shape[2]
    quarter = dim // 4
    total = work.shape[0]
    lanes = work.shape[1] // 2
    bits = total.bit_length() - 1
    depth = count // 2
    z = wide // 2
    x = wide % 2
    members = 2 * count
    me = wide * 2 + narrow
    x_mate = 2 * z + 1 - x
    half = lanes // 2
    tiles = total // lanes

    stem_copy = pltpu.make_async_copy(stem_ref, stem_held, stem_sem)
    stem_copy.start()
    barrier = pltpu.get_barrier_semaphore()
    pl.semaphore_signal(barrier, inc=1, device_id={"cuts": 1 - cut}, device_id_type=MESH)
    for step in range(1, members):
        other = lax.rem(me + step, members)
        pl.semaphore_signal(
            barrier, inc=1, device_id={"wide": other // 2, "narrow": other % 2}, device_id_type=MESH
        )

    started = []
    call = functools.partial
    hops = range(depth)
    far_first = sorted(hops, key=lambda hop: -min(hop, depth - hop))

    def ahead(hop):
        return (z + hop) % depth

    side = z // (depth // 2)
    partner = z + 1 - 2 * (z % 2)
    inner = (z + side) % 2
    level_of = (z, partner, depth // 2 - side, (depth - 1) * (1 - side))
    far_class = 3 - inner
    class_of = (0, 1, far_class, far_class)
    relays = inner == 1

    def row_span(block):
        return pl.ds(pl.multiple_of(block * rows, rows), rows)

    def column_span(block):
        return pl.ds(pl.multiple_of(block * quarter, quarter), quarter)

    def remote(src, dst, send_sem, recv_sem, device_id):
        return pltpu.make_async_remote_copy(
            src_ref=src, dst_ref=dst, send_sem=send_sem, recv_sem=recv_sem,
            device_id=device_id, device_id_type=MESH,
        )

    def guarded(guard, action):
        if guard is None:
            action()
        else:
            pl.when(guard)(action)

    def launch(build, guard=None):
        guarded(guard, lambda: build().start())
        started.append((build, guard))

    def await_recv(build, guard=None):
        guarded(guard, lambda: build().wait_recv())

    holds_left = narrow == 0
    holds_right = narrow == 1
    other_core = {"narrow": 1 - narrow}
    own_columns = column_span(2 * x + cut)

    def left_exchange(which):
        return remote(
            sub_ref.at[which], xbuf.at[which], left_send.at[which], left_recv.at[which],
            {"wide": x_mate, "narrow": 1 - narrow},
        )

    def right_copy(which, across, kind):
        to_x = 1 - x if across else x
        return remote(
            sub_ref.at[which, :, :, column_span(2 * to_x + cut)], ybuf.at[which, :, row_span(wide)],
            right_send.at[which, across, kind], right_recv.at[which, class_of[kind]],
            {"wide": 2 * level_of[kind] + to_x, "narrow": 1 - across},
        )

    def right_block(which, kind):
        return ybuf.at[which, :, row_span(2 * level_of[kind] + xor(x, 1 - narrow))]

    def right_relay(which, kind):
        block = right_block(which, kind)
        return remote(
            block, block, relay_send.at[0, which, kind], right_recv.at[which, kind], {"wide": 2 * partner + x}
        )

    def left_own(which):
        return pltpu.make_async_copy(sub_ref.at[which], xbuf.at[which], own_sem.at[which])

    def right_own(which):
        return pltpu.make_async_copy(
            sub_ref.at[which, :, :, own_columns], ybuf.at[which, :, row_span(wide)], own_sem.at[which]
        )

    def pair_copy(which, hop):
        block = right_block(which, hop)
        return remote(block, block, pair_send.at[which, hop], pair_recv.at[which, hop], other_core)

    def b_block(which, level, far_x, far_cut):
        from_x = 1 - x if far_x else x
        from_cut = 1 - cut if far_cut else cut
        return bbuf.at[
            which, :, row_span(2 * level + xor(from_x, narrow)), column_span(2 * from_x + from_cut)
        ]

    def zb_copy(which, kind):
        block = b_block(which, z, 0, 0)
        return remote(
            block, block, zb_send.at[which, kind], zb_recv.at[which, class_of[kind]],
            {"wide": 2 * level_of[kind] + x},
        )

    def zb_relay(which, kind):
        block = b_block(which, level_of[kind], 0, 0)
        return remote(
            block, block, relay_send.at[1, which, kind], zb_recv.at[which, kind], {"wide": 2 * partner + x}
        )

    def xb_copy(which, far_cut, hop):
        block = b_block(which, level_of[hop], 0, far_cut)
        return remote(
            block, block, xb_send.at[which, far_cut, hop], xb_recv.at[which, far_cut, hop], {"wide": x_mate}
        )

    def yb_copy(which, far_x, hop):
        block = b_block(which, level_of[hop], far_x, 0)
        return remote(
            block, block, yb_send.at[which, far_x, hop], yb_recv.at[which, far_x, hop], {"cuts": 1 - cut}
        )

    def pb_copy(which, far_x, far_cut, hop):
        block = b_block(which, level_of[hop], far_x, far_cut)
        return remote(
            block, block, pb_send.at[which, far_x, far_cut, hop], pb_recv.at[which, far_x, far_cut, hop],
            other_core,
        )

    def open_exchange(which):
        launch(call(left_exchange, which), holds_left)
        guarded(holds_left, lambda: left_own(which).start())
        for kind in (3, 2, 1, 0) if which in WHOLE_WAY else (2, 1, 0):
            launch(call(right_copy, which, 1, kind), holds_right)
            if kind:
                launch(call(right_copy, which, 0, kind), holds_right)
        guarded(holds_right, lambda: right_own(which).start())

    def merge(which):
        guarded(holds_left, lambda: left_own(which).wait())
        await_recv(call(left_exchange, which), holds_right)
        for hop in hops:
            await_recv(call(pair_copy, which, hop))
        left = jnp.concatenate([xbuf[which, part] for part in range(2)], axis=0)
        right = jnp.concatenate([ybuf[which, part] for part in range(2)], axis=1)
        both = jnp.dot(left, right, preferred_element_type=jnp.float32)
        real = both[:rows, :quarter] - both[rows:, quarter:]
        imag = both[:rows, quarter:] + both[rows:, :quarter]
        span = row_span(2 * z + xor(x, narrow))
        bbuf[which, 0, span, own_columns] = real.astype(jnp.bfloat16)
        bbuf[which, 1, span, own_columns] = imag.astype(jnp.bfloat16)
        for kind in (2, 1):
            launch(call(zb_copy, which, kind))
        spread(which, 0)

    def spread(which, hop):
        launch(call(yb_copy, which, 0, hop))
        launch(call(xb_copy, which, 0, hop))
        launch(call(pb_copy, which, 0, 0, hop))

    def over_x(which, hop):
        return (hop, which) in CORNERS_OVER_X

    def take_xb(which, far_cut, hop):
        await_recv(call(xb_copy, which, far_cut, hop))
        if not far_cut and not over_x(which, hop):
            launch(call(yb_copy, which, 1, hop))
        launch(call(pb_copy, which, 1, far_cut, hop))

    def take_yb(which, far_x, hop):
        await_recv(call(yb_copy, which, far_x, hop))
        if not far_x and over_x(which, hop):
            launch(call(xb_copy, which, 1, hop))
        launch(call(pb_copy, which, far_x, 1, hop))

    def take_sides(which, hop):
        take_xb(which, 0, hop)
        take_yb(which, 0, hop)

    def take_corner(which, hop):
        if over_x(which, hop):
            take_xb(which, 1, hop)
        else:
            take_yb(which, 1, hop)

    def take_right_piece(which, hop):
        if hop == 0:
            guarded(holds_right, lambda: right_own(which).wait())
            await_recv(call(right_copy, which, 1, 0), holds_left)
        else:
            await_recv(call(right_relay, which, hop))
            if hop > 1 and which not in WHOLE_WAY:
                launch(call(right_relay, which, hop), relays)
        launch(call(pair_copy, which, hop))

    def take_z(which, hop):
        await_recv(call(zb_relay, which, hop))
        if hop > 1:
            launch(call(zb_relay, which, hop), relays)
        spread(which, hop)

    near_first = list(reversed(far_first))

    def complete(which):
        for hop in hops:
            for far_x in (0, 1):
                for far_cut in (0, 1):
                    await_recv(call(pb_copy, which, far_x, far_cut, hop))

    width = dim.bit_length() - 1
    narrow_place = bits - 1 - (count.bit_length() - 1)

    def named_place(which, slot):
        bit = places_ref[which, slot]
        return bit + jnp.where(bit < LBITS, -lane_bits, narrow_place - LBITS)

    places = [[named_place(which, slot) for slot in range(width)] for which in range(branches)]

    def free_place(which):
        rest = bits * (bits - 1) // 2
        for slot in range(width):
            rest = rest - places[which][slot]
        return rest

    def bit_at(values, position):
        return jnp.bitwise_and(jnp.right_shift(values, position), 1)

    def gathered_place(which, values):
        found = jnp.left_shift(bit_at(values, free_place(which)), width)
        for slot in range(width):
            found = found + jnp.left_shift(
                bit_at(values, places[which][slot]), width - 1 - slot
            )
        return found

    def natural_place(which, values):
        found = jnp.left_shift(bit_at(values, width), free_place(which))
        for slot in range(width):
            found = found + jnp.left_shift(
                bit_at(values, width - 1 - slot), places[which][slot]
            )
        return found

    step = min(256, total)
    line = lax.broadcasted_iota(jnp.int32, (1, total), 1)

    def onehot(first, size, goal):
        index = lax.broadcasted_iota(jnp.int32, (size, total), 0) + first
        return (index == goal).astype(jnp.float32).astype(jnp.bfloat16)

    def product(left, right, left_axis, right_axis):
        return lax.dot_general(
            left, right, (((left_axis,), (right_axis,)), ((), ())),
            preferred_element_type=jnp.float32,
        )

    def permute(source, source_axis, goal):
        for first in range(0, total, step):
            work[first:first + step, :] = product(
                onehot(first, step, goal), source, 1, source_axis
            ).astype(jnp.bfloat16)

    def contract(which):
        branch = jnp.concatenate([bbuf[which, part] for part in range(2)], axis=1)
        for first in range(0, total, dim):
            data = work[first:first + dim, :]
            spun = jnp.concatenate([-data[:, lanes:], data[:, :lanes]], axis=1)
            both = jnp.concatenate([data, spun], axis=0)
            prod[first:first + dim, :] = jnp.dot(
                branch, both, preferred_element_type=jnp.float32
            ).astype(jnp.bfloat16)

    def swap_targets(round_no, hop):
        source, target = ((send_in, recv_in), (send_out, recv_out))[round_no]
        piece = source.shape[0] // members
        for turn in range(4):
            across, other_side = turn // 2, turn % 2
            if hop == 0 and turn == 0:
                continue
            to_x = x if across == 0 else 1 - x
            to_core = narrow if other_side == 0 else 1 - narrow
            to_wide = 2 * ahead(hop) + to_x
            other = 2 * to_wide + to_core
            yield remote(
                source.at[pl.ds(pl.multiple_of(other * piece, piece), piece)],
                target.at[pl.ds(pl.multiple_of(me * piece, piece), piece)],
                swap_send.at[round_no, 4 * hop + turn],
                swap_recv.at[round_no, 4 * hop + turn],
                {"wide": to_wide, "narrow": to_core},
            )

    def swap_start(round_no, hop):
        for copy in swap_targets(round_no, hop):
            copy.start()

    def swap_wait(round_no):
        for hop in far_first:
            for copy in swap_targets(round_no, hop):
                copy.wait_recv()

    def keep_own(source, target):
        piece = source.shape[0] // members
        mine = pl.ds(pl.multiple_of(me * piece, piece), piece)
        target[mine, :] = source[mine, :]

    def pack():
        sides = [
            stem_held[pl.ds(part, total, stride=2), :].T.reshape(members, 1, sublanes, total)
            for part in range(2)
        ]
        send_in[...] = jnp.concatenate(sides, axis=1).reshape(2 * lanes, total).astype(jnp.bfloat16)
        keep_own(send_in, recv_in)

    def arrange():
        blocks = recv_in[...].astype(jnp.float32).reshape(members, 2, sublanes, total)
        return jnp.concatenate(
            [blocks[:, part].reshape(lanes, total) for part in range(2)], axis=0
        ).astype(jnp.bfloat16)

    def mix(low, high):
        return (
            jnp.concatenate([low[..., :half], high[..., :half]], axis=-1),
            jnp.concatenate([low[..., half:], high[..., half:]], axis=-1),
        )

    def turn_over():
        goal = natural_place(0, line)
        for first in range(0, total, step):
            turned[:, first:first + step] = product(prod[...], onehot(first, step, goal), 0, 1)
        for tile in range(tiles):
            block = turned[:, tile * lanes:(tile + 1) * lanes].reshape(2, count, 2, sublanes, lanes)
            for side, mixed in enumerate(mix(block[:, :, 0], block[:, :, 1])):
                for part in range(2):
                    first = ((part * 2 + side) * tiles + tile) * sublanes
                    flipped[first:first + sublanes, :] = jnp.concatenate(
                        [mixed[part, column] for column in range(count)], axis=1
                    )

    def hand_out(hop, goal):
        span = 2 * lanes
        first = ahead(hop) * span
        level = product(prod[...], onehot(first, span, goal), 0, 1)
        piece = send_out.shape[0] // members
        for to_x in range(2):
            block = level[:, to_x * lanes:(to_x + 1) * lanes].reshape(2, 2, half, lanes)
            for side, mixed in enumerate(mix(block[:, 0], block[:, 1])):
                other = 2 * (2 * ahead(hop) + to_x) + side
                send_out[pl.ds(pl.multiple_of(other * piece, piece), piece), :] = mixed.reshape(
                    piece, lanes
                ).astype(jnp.bfloat16)
        swap_start(1, hop)

    def write():
        for tile in range(tiles):
            for part in range(2):
                first = (part * tiles + tile) * sublanes
                block = jnp.concatenate(
                    [
                        recv_out[
                            member * lanes + first // 16 * 16:member * lanes + first // 16 * 16 + 16, :
                        ].astype(jnp.float32)[first % 16:first % 16 + sublanes]
                        for member in range(members)
                    ],
                    axis=0,
                )
                out_ref[pl.ds(2 * tile * lanes + part, lanes, stride=2), :] = block.T

    stem_copy.wait()
    pack()
    pl.semaphore_wait(barrier, members)
    swap_start(0, 1)
    open_exchange(1)
    take_right_piece(1, 0)
    open_exchange(0)
    open_exchange(2)
    take_right_piece(1, 3)
    take_right_piece(1, 2)
    take_right_piece(1, 1)
    merge(1)
    take_right_piece(0, 0)
    take_right_piece(0, 1)
    take_right_piece(0, 3)
    take_right_piece(0, 2)
    take_right_piece(2, 1)
    take_right_piece(2, 0)
    merge(0)
    take_right_piece(2, 2)
    take_right_piece(2, 3)
    take_z(1, 2)
    merge(2)
    take_z(0, 2)
    take_z(1, 3)
    take_sides(0, 0)
    take_z(2, 2)
    take_z(1, 1)
    take_sides(1, 2)
    take_z(0, 3)
    take_sides(0, 2)
    take_z(0, 1)
    take_sides(2, 2)
    take_sides(1, 3)
    take_z(2, 1)
    swap_start(0, 2)
    take_sides(1, 0)
    take_sides(1, 1)
    take_corner(0, 0)
    take_z(2, 3)
    take_corner(0, 2)
    swap_start(0, 3)
    swap_start(0, 0)
    take_sides(0, 1)
    take_sides(0, 3)
    take_sides(2, 1)
    take_corner(0, 1)
    take_corner(1, 0)
    take_sides(2, 0)
    take_corner(0, 3)
    take_corner(2, 2)
    take_sides(2, 3)
    take_corner(1, 1)
    take_corner(2, 1)
    take_corner(1, 2)
    take_corner(1, 3)
    complete(0)
    swap_wait(0)
    permute(arrange(), 1, gathered_place(0, line))
    contract(0)
    turn_over()
    take_corner(2, 3)
    take_corner(2, 0)
    complete(1)
    permute(flipped[...].astype(jnp.bfloat16), 1, gathered_place(1, line))
    contract(1)
    permute(prod[...], 0, gathered_place(2, natural_place(1, line)))
    complete(2)
    contract(2)
    goal = natural_place(2, line)
    for hop in far_first:
        hand_out(hop, goal)
    keep_own(send_out, recv_out)
    swap_wait(1)
    write()


    for hop in hops:
        for round_no in range(2):
            for copy in swap_targets(round_no, hop):
                copy.wait_send()
    for build, guard in started:
        guarded(guard, lambda: build().wait_send())


def shards_in_kernel(stem_tensor, sub_branches, branch_bits):
    count = lax.axis_size("wide")
    depth = count // 2
    lanes = 2**lane_bits
    total = stem_tensor.shape[1] // lanes
    dim = sub_branches.shape[-1]
    stem = stem_tensor.reshape(2, total, lanes).transpose(1, 0, 2).reshape(2 * total, lanes)
    vmem = pl.BlockSpec(memory_space=pltpu.VMEM)
    hbm = pl.BlockSpec(memory_space=pl.ANY)
    each = (BRANCHES, depth)
    semaphores = [pltpu.SemaphoreType.DMA(()), pltpu.SemaphoreType.DMA((BRANCHES,))]
    for sent, received in (
        ((BRANCHES,), (BRANCHES,)), ((BRANCHES, 2, depth), each), (each, each), (each, each),
        ((BRANCHES, 2, depth),) * 2, ((BRANCHES, 2, depth),) * 2, ((BRANCHES, 2, 2, depth),) * 2, ((2, 2 * count),) * 2,
    ):
        semaphores += [pltpu.SemaphoreType.DMA(sent), pltpu.SemaphoreType.DMA(received)]
    semaphores.insert(8, pltpu.SemaphoreType.DMA((2,) + each))
    half_size = jnp.bfloat16
    result = pl.pallas_call(
        functools.partial(stem_kernel, count),
        out_shape=jax.ShapeDtypeStruct((2 * total, lanes), jnp.float32),
        in_specs=[pl.BlockSpec(memory_space=pltpu.SMEM), hbm, hbm],
        out_specs=vmem,
        scratch_shapes=[
            pltpu.VMEM((BRANCHES,) + sub_branches.shape[2:], half_size),
            pltpu.VMEM((BRANCHES, 2, dim, dim // 4), half_size),
            pltpu.VMEM((BRANCHES, 2, dim, dim), half_size),
            pltpu.VMEM((total, 2 * lanes), half_size),
            pltpu.VMEM((total, 2 * lanes), half_size),
            pltpu.VMEM((2 * lanes, total), jnp.float32),
            pltpu.VMEM((2 * lanes, total), jnp.float32),
            pltpu.VMEM((2 * lanes, total), half_size),
            pltpu.VMEM((2 * lanes, total), half_size),
            pltpu.VMEM((2 * total, lanes), half_size),
            pltpu.VMEM((2 * total, lanes), half_size),
            pltpu.VMEM((2 * total, lanes), jnp.float32),
        ] + semaphores,
        compiler_params=pltpu.CompilerParams(collective_id=0, has_side_effects=True),
    )(branch_bits, stem, sub_branches[:, 0])
    return result.reshape(total, 2, lanes).transpose(1, 0, 2).reshape(2, -1)


sublane_tile = 16


def solution(mesh):
    in_specs = (P(None, ("cuts", "wide", "narrow")), P(None, "narrow", None, "wide", None), P())
    out_specs = P(None, ("cuts", "wide", "narrow"))

    def run(stem_tensor, sub_branches, branch_bits):
        whole_tiles = sub_branches.shape[3] % sublane_tile == 0 and mesh.shape["cuts"] == 2
        whole_groups = 2 * mesh.shape["wide"] * sublanes == 2**lane_bits
        body = shards_in_kernel if whole_tiles and whole_groups else shards
        return body(stem_tensor, sub_branches, branch_bits)

    return jax.shard_map(run, mesh=mesh, in_specs=in_specs, out_specs=out_specs, check_vma=False)
```

time: 63.5 us -> 60.4 us (0.951)
  Pallas kernels: 61 us -> 57.9 us
    pallas_call x1, Pallas kernels: 61 us -> 57.9 us  [shards_in_kernel(): pl.pallas_call(functools.partial(stem_kernel, count), out_shape=jax.Shape...]
where the time goes in v1:
time: 60.4 us; the launch traced here: 60.2 us
  Pallas kernels  57.9 us (96%)
  local copies, waits for them, and re-layouts  2.26 us (4%)
    pallas_call x1, Pallas kernels, shards_in_kernel(): pl.pallas_call(functools.partial(stem_kernel, count), out_shape=jax.Shape...  57.9 us
    unnamed x1, local copies, waits for them, and re-layouts  2.26 us

profile of v1, /device:TPU:9, one launch (start us, length us, event | category | flops | bytes accessed | tf_op | source)
XLA Modules:
  0.0 60.2 jit_solution(18002174729979504097)
XLA Ops:
  0.0 57.9 %shard_map.37 = f32[2048,128]{1,0:T(8,128)} custom-call(s32[3,9]{1,0:T(4,128)} %places_ref.1, f32[2048,128]{1,0:T(8,128)} %bitcast.12, bf16[3,2,64,512]{3,2,1,0:T(8,128)(2,1)} %bitcast.13), custom_call_target="tpu_custom_call" | custom-call | tf_op jit(solution)/shard_map/pallas_call | solution.py:658
  57.9 2.3 %copy.7 = f32[2,131072]{1,0:T(2,128)} copy(f32[2,131072]{1,0:T(2,128)} %bitcast.11) | data formatting | bytes 2097152

commit v2 on v1

--- a/solution.py
+++ b/solution.py
@@ -14,8 +14,12 @@
 
 lane_bits = 7
 sublanes = 8
-CORNERS_OVER_X = ((0, 2), (2, 0), (2, 2))
+kernel_vmem = 32 * 2**20
+CORNERS_OVER_X = ((2, 0), (2, 2))
 WHOLE_WAY = ()
+SIDEWAYS_FIRST = ()
+CORNERS_DIRECT = ()
+LEVELS_DIRECT = ()
 
 
 def partner(value, axis, stride):
@@ -159,7 +163,7 @@
 
 
 def stem_kernel(
-    count, places_ref, stem_ref, sub_ref, out_ref,
+    count, bits_ref, stem_ref, sub_ref, out_ref, places_ref, places_sem,
     xbuf, ybuf, bbuf, work, prod, turned, flipped, send_in, recv_in, send_out, recv_out, stem_held,
     stem_sem, own_sem, left_send, left_recv, right_send, right_recv, pair_send, pair_recv,
     relay_send, zb_send, zb_recv, xb_send, xb_recv, yb_send, yb_recv, pb_send, pb_recv,
@@ -186,8 +190,12 @@
 
     stem_copy = pltpu.make_async_copy(stem_ref, stem_held, stem_sem)
     stem_copy.start()
+    places_copy = pltpu.make_async_copy(bits_ref, places_ref, places_sem)
+    places_copy.start()
     barrier = pltpu.get_barrier_semaphore()
-    pl.semaphore_signal(barrier, inc=1, device_id={"cuts": 1 - cut}, device_id_type=MESH)
+    corner = {"wide": x_mate, "cuts": 1 - cut}
+    for target in ({"cuts": 1 - cut}, corner):
+        pl.semaphore_signal(barrier, inc=1, device_id=target, device_id_type=MESH)
     for step in range(1, members):
         other = lax.rem(me + step, members)
         pl.semaphore_signal(
@@ -257,6 +265,13 @@
     def right_block(which, kind):
         return ybuf.at[which, :, row_span(2 * level_of[kind] + xor(x, 1 - narrow))]
 
+    def right_pass(which, kind):
+        block = right_block(which, 0)
+        return remote(
+            block, block, right_send.at[which, 1, kind], right_recv.at[which, class_of[kind]],
+            {"wide": 2 * level_of[kind] + x},
+        )
+
     def right_relay(which, kind):
         block = right_block(which, kind)
         return remote(
@@ -318,7 +333,8 @@
         launch(call(left_exchange, which), holds_left)
         guarded(holds_left, lambda: left_own(which).start())
         for kind in (3, 2, 1, 0) if which in WHOLE_WAY else (2, 1, 0):
-            launch(call(right_copy, which, 1, kind), holds_right)
+            if kind == 0 or which not in SIDEWAYS_FIRST:
+                launch(call(right_copy, which, 1, kind), holds_right)
             if kind:
                 launch(call(right_copy, which, 0, kind), holds_right)
         guarded(holds_right, lambda: right_own(which).start())
@@ -336,11 +352,17 @@
         span = row_span(2 * z + xor(x, narrow))
         bbuf[which, 0, span, own_columns] = real.astype(jnp.bfloat16)
         bbuf[which, 1, span, own_columns] = imag.astype(jnp.bfloat16)
-        for kind in (2, 1):
+        for kind in (3, 2, 1) if which in LEVELS_DIRECT else (2, 1):
             launch(call(zb_copy, which, kind))
         spread(which, 0)
 
+    def corner_copy(which, hop):
+        block = b_block(which, level_of[hop], 0, 0)
+        return remote(block, block, yb_send.at[which, 1, hop], yb_recv.at[which, 1, hop], corner)
+
     def spread(which, hop):
+        if (hop, which) in CORNERS_DIRECT:
+            launch(call(corner_copy, which, hop))
         launch(call(yb_copy, which, 0, hop))
         launch(call(xb_copy, which, 0, hop))
         launch(call(pb_copy, which, 0, 0, hop))
@@ -350,7 +372,7 @@
 
     def take_xb(which, far_cut, hop):
         await_recv(call(xb_copy, which, far_cut, hop))
-        if not far_cut and not over_x(which, hop):
+        if not far_cut and not over_x(which, hop) and (hop, which) not in CORNERS_DIRECT:
             launch(call(yb_copy, which, 1, hop))
         launch(call(pb_copy, which, 1, far_cut, hop))
 
@@ -374,6 +396,9 @@
         if hop == 0:
             guarded(holds_right, lambda: right_own(which).wait())
             await_recv(call(right_copy, which, 1, 0), holds_left)
+            if which in SIDEWAYS_FIRST:
+                for kind in (2, 1):
+                    launch(call(right_pass, which, kind), holds_left)
         else:
             await_recv(call(right_relay, which, hop))
             if hop > 1 and which not in WHOLE_WAY:
@@ -382,7 +407,7 @@
 
     def take_z(which, hop):
         await_recv(call(zb_relay, which, hop))
-        if hop > 1:
+        if hop > 1 and which not in LEVELS_DIRECT:
             launch(call(zb_relay, which, hop), relays)
         spread(which, hop)
 
@@ -395,6 +420,7 @@
                     await_recv(call(pb_copy, which, far_x, far_cut, hop))
 
     width = dim.bit_length() - 1
+    places_copy.wait()
     narrow_place = bits - 1 - (count.bit_length() - 1)
 
     def named_place(which, slot):
@@ -537,24 +563,9 @@
                 ).astype(jnp.bfloat16)
         swap_start(1, hop)
 
-    def write():
-        for tile in range(tiles):
-            for part in range(2):
-                first = (part * tiles + tile) * sublanes
-                block = jnp.concatenate(
-                    [
-                        recv_out[
-                            member * lanes + first // 16 * 16:member * lanes + first // 16 * 16 + 16, :
-                        ].astype(jnp.float32)[first % 16:first % 16 + sublanes]
-                        for member in range(members)
-                    ],
-                    axis=0,
-                )
-                out_ref[pl.ds(2 * tile * lanes + part, lanes, stride=2), :] = block.T
-
     stem_copy.wait()
     pack()
-    pl.semaphore_wait(barrier, members)
+    pl.semaphore_wait(barrier, members + 1)
     swap_start(0, 1)
     open_exchange(1)
     take_right_piece(1, 0)
@@ -563,13 +574,13 @@
     take_right_piece(1, 3)
     take_right_piece(1, 2)
     take_right_piece(1, 1)
+    take_right_piece(2, 0)
     merge(1)
     take_right_piece(0, 0)
     take_right_piece(0, 1)
     take_right_piece(0, 3)
     take_right_piece(0, 2)
     take_right_piece(2, 1)
-    take_right_piece(2, 0)
     merge(0)
     take_right_piece(2, 2)
     take_right_piece(2, 3)
@@ -585,11 +596,11 @@
     take_sides(0, 2)
     take_z(0, 1)
     take_sides(2, 2)
-    take_sides(1, 3)
     take_z(2, 1)
     swap_start(0, 2)
     take_sides(1, 0)
     take_sides(1, 1)
+    take_sides(1, 3)
     take_corner(0, 0)
     take_z(2, 3)
     take_corner(0, 2)
@@ -626,7 +637,7 @@
         hand_out(hop, goal)
     keep_own(send_out, recv_out)
     swap_wait(1)
-    write()
+    out_ref[...] = recv_out[...]
 
 
     for hop in hops:
@@ -635,6 +646,32 @@
                 copy.wait_send()
     for build, guard in started:
         guarded(guard, lambda: build().wait_send())
+
+
+def write_kernel(parts_ref, out_ref, held, sems):
+    lanes = held.shape[1]
+    members = parts_ref.shape[0] // lanes
+    tiles = lanes // (2 * sublanes)
+    copies = []
+    for tile in range(tiles):
+        for part in range(2):
+            first = (part * tiles + tile) * sublanes
+            start = first // 16 * 16
+            block = jnp.concatenate(
+                [
+                    parts_ref[member * lanes + start:member * lanes + start + 16, :].astype(jnp.float32)[
+                        first - start:first - start + sublanes
+                    ]
+                    for member in range(members)
+                ],
+                axis=0,
+            )
+            held[pl.ds(2 * tile * lanes + part, lanes, stride=2), :] = block.T
+        span = pl.ds(2 * tile * lanes, 2 * lanes)
+        copies.append(pltpu.make_async_copy(held.at[span], out_ref.at[span], sems.at[tile]))
+        copies[-1].start()
+    for copy in copies:
+        copy.wait()
 
 
 def shards_in_kernel(stem_tensor, sub_branches, branch_bits):
@@ -657,10 +694,12 @@
     half_size = jnp.bfloat16
     result = pl.pallas_call(
         functools.partial(stem_kernel, count),
-        out_shape=jax.ShapeDtypeStruct((2 * total, lanes), jnp.float32),
-        in_specs=[pl.BlockSpec(memory_space=pltpu.SMEM), hbm, hbm],
+        out_shape=jax.ShapeDtypeStruct((2 * total, lanes), half_size),
+        in_specs=[pl.BlockSpec(memory_space=pltpu.MemorySpace.HBM), hbm, hbm],
         out_specs=vmem,
         scratch_shapes=[
+            pltpu.SMEM(branch_bits.shape, jnp.int32),
+            pltpu.SemaphoreType.DMA(()),
             pltpu.VMEM((BRANCHES,) + sub_branches.shape[2:], half_size),
             pltpu.VMEM((BRANCHES, 2, dim, dim // 4), half_size),
             pltpu.VMEM((BRANCHES, 2, dim, dim), half_size),
@@ -674,8 +713,20 @@
             pltpu.VMEM((2 * total, lanes), half_size),
             pltpu.VMEM((2 * total, lanes), jnp.float32),
         ] + semaphores,
-        compiler_params=pltpu.CompilerParams(collective_id=0, has_side_effects=True),
-    )(branch_bits, stem, sub_branches[:, 0])
+        compiler_params=pltpu.CompilerParams(
+            collective_id=0, has_side_effects=True, vmem_limit_bytes=kernel_vmem
+        ),
+    )(*[pltpu.with_memory_space_constraint(v, pltpu.MemorySpace.HBM) for v in (branch_bits, stem, sub_branches[:, 0])])
+    result = pl.pallas_call(
+        write_kernel,
+        out_shape=jax.ShapeDtypeStruct((2 * total, lanes), jnp.float32),
+        in_specs=[vmem],
+        out_specs=hbm,
+        scratch_shapes=[
+            pltpu.VMEM((2 * total, lanes), jnp.float32), pltpu.SemaphoreType.DMA((total // lanes,))
+        ],
+        compiler_params=pltpu.CompilerParams(vmem_limit_bytes=kernel_vmem),
+    )(result)
     return result.reshape(total, 2, lanes).transpose(1, 0, 2).reshape(2, -1)
 
 

time: 60.4 us -> 57 us (0.944)
  local copies, waits for them, and re-layouts: 2.26 us -> 0 us
  Pallas kernels: 57.9 us -> 56.5 us
    pallas_call x1, Pallas kernels: 57.9 us -> 55.3 us  [shards_in_kernel(): pl.pallas_call(functools.partial(stem_kernel, count), out_shape=jax.Shape...]
    unnamed x1 -> x0, local copies, waits for them, and re-layouts: 2.26 us -> none
    pallas_call x0 -> x1, Pallas kernels: none -> 1.13 us  [shards_in_kernel(): pl.pallas_call(write_kernel, out_shape=jax.ShapeDtypeStruct((2 * total, l...]
where the time goes in v2:
time: 57 us; the launch traced here: 56.5 us
  Pallas kernels  56.5 us (99%)
    pallas_call x1, Pallas kernels, shards_in_kernel(): pl.pallas_call(functools.partial(stem_kernel, count), out_shape=jax.Shape...  55.3 us

profile of v2, /device:TPU:9, one launch (start us, length us, event | category | flops | bytes accessed | tf_op | source)
XLA Modules:
  0.0 56.5 jit_solution(16270300432332218272)
XLA Ops:
  0.0 55.3 %shard_map.37.parts_ref = bf16[2048,128]{1,0:T(8,128)(2,1)S(1)} custom-call(s32[3,9]{1,0:T(4,128)} %bits_ref.1, f32[2048,128]{1,0:T(8,128)} %bitcast.11, bf16[3,2,64,512]{3,2,1,0:T(8,128)(2,1)} %bitcast.12), custom_call_target="tpu_custom_call" | custom-call | tf_op jit(solution)/shard_map/pallas_call | solution.py:695
  55.3 1.1 %shard_map.38 = f32[2048,128]{1,0:T(8,128)} custom-call(bf16[2048,128]{1,0:T(8,128)(2,1)S(1)} %shard_map.37.parts_ref), custom_call_target="tpu_custom_call" | custom-call | tf_op jit(solution)/shard_map/pallas_call | solution.py:720

commit v3 on v2

--- a/solution.py
+++ b/solution.py
@@ -193,14 +193,14 @@
     places_copy = pltpu.make_async_copy(bits_ref, places_ref, places_sem)
     places_copy.start()
     barrier = pltpu.get_barrier_semaphore()
+    for step in sorted(range(1, members), key=lambda step: -min(step, members - step)):
+        other = lax.rem(me + step, members)
+        pl.semaphore_signal(
+            barrier, inc=1, device_id={"wide": other // 2, "narrow": other % 2}, device_id_type=MESH
+        )
     corner = {"wide": x_mate, "cuts": 1 - cut}
     for target in ({"cuts": 1 - cut}, corner):
         pl.semaphore_signal(barrier, inc=1, device_id=target, device_id_type=MESH)
-    for step in range(1, members):
-        other = lax.rem(me + step, members)
-        pl.semaphore_signal(
-            barrier, inc=1, device_id={"wide": other // 2, "narrow": other % 2}, device_id_type=MESH
-        )
 
     started = []
     call = functools.partial
@@ -624,10 +624,10 @@
     permute(arrange(), 1, gathered_place(0, line))
     contract(0)
     turn_over()
+    permute(flipped[...].astype(jnp.bfloat16), 1, gathered_place(1, line))
     take_corner(2, 3)
     take_corner(2, 0)
     complete(1)
-    permute(flipped[...].astype(jnp.bfloat16), 1, gathered_place(1, line))
     contract(1)
     permute(prod[...], 0, gathered_place(2, natural_place(1, line)))
     complete(2)

time: 57 us -> 57 us (level)
  no operation moved by 1% of the time
where the time goes in v3:
time: 57 us; the launch traced here: 56.8 us
  Pallas kernels  56.8 us (100%)
    pallas_call x1, Pallas kernels, shards_in_kernel(): pl.pallas_call(functools.partial(stem_kernel, count), out_shape=jax.Shape...  55.7 us

profile of v3, /device:TPU:9, one launch (start us, length us, event | category | flops | bytes accessed | tf_op | source)
XLA Modules:
  0.0 56.8 jit_solution(15840713413986624947)
XLA Ops:
  0.0 55.7 %shard_map.37.parts_ref = bf16[2048,128]{1,0:T(8,128)(2,1)S(1)} custom-call(s32[3,9]{1,0:T(4,128)} %bits_ref.1, f32[2048,128]{1,0:T(8,128)} %bitcast.11, bf16[3,2,64,512]{3,2,1,0:T(8,128)(2,1)} %bitcast.12), custom_call_target="tpu_custom_call" | custom-call | tf_op jit(solution)/shard_map/pallas_call | solution.py:695
  55.7 1.1 %shard_map.38 = f32[2048,128]{1,0:T(8,128)} custom-call(bf16[2048,128]{1,0:T(8,128)(2,1)S(1)} %shard_map.37.parts_ref), custom_call_target="tpu_custom_call" | custom-call | tf_op jit(solution)/shard_map/pallas_call | solution.py:720
